TPU v7x, 32 devices: a whole 2x2x4 slice. The times are simulated.
32 devices in a mesh: line: 16 (over z, y, x), sec: 2 (over core).
Axes of the slice: x: 2, y: 2, z: 4, core: 2. Of those that a mesh axis runs over, the one named last changes fastest.
Arguments:
- right_side: float32 [16, 2, 256, 256], P('line', 'sec'), may hold values from -80 to 80
- inverse_diag: float32 [16, 2, 256, 256], P('line', 'sec'), may hold values from -3 to 3
- couplings: float32 [16, 2, 2, 256, 256], P('line', 'sec'), may hold values from -0.5 to 0.5
- neighbors: int32 [16, 2, 2], P('line', 'sec'), may hold values from -1 to 0, as said below
Outputs:
- panel: float32 [16, 2, 256, 256], P('line', 'sec')
- factor: float32 [256, 256], replicated
Inputs may be any that keep to these rules, and one draw needn't show every extreme that they name: `neighbors`: every entry is -1 or a section lower than its own; slot 0 of every section after the first names the section just before it; the first section's entries are all -1.
All inputs are finite; a program needn't handle non-finite values.
Results may differ from a plain program's by a relative error of at most 0.0001.
Values sent between devices are 32-bit elements; how exact they have to be, the bound alone decides.
No kernel may reach another device: no remote copies, remote signals or barrier semaphores. Data moves between devices by JAX's collectives and lax.ppermute only.
A program may use at most 64 MiB of HBM per device.

v0:
```python
import jax
import jax.numpy as jnp
from jax import lax
from jax.sharding import PartitionSpec as P


def broadcast(array, axis, root):
    mine = lax.axis_index(axis) == root
    return lax.psum(jnp.where(mine, array, jnp.zeros_like(array)), axis)


def exact_dot(left, right):
    return jnp.dot(left, right, precision=lax.Precision.HIGHEST, preferred_element_type=jnp.float32)


def solve_here(acc, inverse, mine):
    return lax.cond(
        mine, lambda value: exact_dot(inverse, value), lambda value: jnp.zeros_like(value), acc
    )


def absorb(acc, coupled, links, anchor, arrived):
    for slot in range(coupled.shape[0]):
        matrix = coupled[slot]
        acc = lax.cond(
            links[slot] == anchor,
            lambda value, mat=matrix: value - exact_dot(mat, arrived),
            lambda value: value,
            acc,
        )
    return acc


def gram_sum(matrix):
    local = exact_dot(matrix.T, matrix)
    return lax.psum(local, ("line", "sec"))


def upper_factor(matrix, total):
    lower = jnp.linalg.cholesky(gram_sum(matrix) / total)
    normed = jax.scipy.linalg.solve_triangular(lower, matrix.T, lower=True).T
    return (normed, lower.T)


def shards(right_side, inverse_diag, couplings, neighbors):
    target = right_side[0, 0]
    inverse = inverse_diag[0, 0]
    coupled = couplings[0, 0]
    links = neighbors[0, 0]
    section = lax.axis_index("sec")
    count = lax.axis_size("sec")
    acc = target
    solved = jnp.zeros_like(target)
    for anchor in range(count):
        mine = section == anchor
        candidate = solve_here(acc, inverse, mine)
        arrived = broadcast(candidate, "sec", anchor)
        solved = jnp.where(mine, arrived, solved)
        acc = absorb(acc, coupled, links, anchor, arrived)
    total = jnp.float32(lax.axis_size("line") * count * target.shape[0])
    second, factor = upper_factor(solved, total)
    return (second[None, None], factor)


def solution(mesh):
    placed = (
        P("line", "sec", None, None),
        P("line", "sec", None, None),
        P("line", "sec", None, None, None),
        P("line", "sec", None),
    )
    return jax.shard_map(
        shards,
        mesh=mesh,
        in_specs=placed,
        out_specs=(P("line", "sec", None, None), P()),
        check_vma=False,
    )
```

profile of v0, /device:TPU:0, one launch (start us, length us, event | category | flops | bytes accessed | tf_op | source)
XLA Modules:
  0.0 260.2 jit_solution(11902350834891242868)
XLA Ops:
  7.2 0.0 copy-start.1
  7.2 0.0 all-reduce.5.cloned.1.call-start
  7.2 1.0 copy.33
  8.2 0.0 copy-done.1
  8.2 0.4 conditional.4
  8.2 0.4 fusion.19
  8.6 0.0 copy-start.4
  8.6 0.7 broadcast_select_fusion.1
  9.3 0.0 all-reduce.5.cloned.1.call-update
  9.4 0.0 all-reduce.7.cloned.1.call-start
  9.4 0.0 copy-start.5
  9.4 0.6 copy-done.5
  10.1 0.6 fusion.18
  11.9 20.0 %all-reduce.5.cloned.1.call-done = f32[256,256]{1,0:T(8,128)} async-done(((f32[256,256]{1,0:T(8,128)}), f32[256,256]{1,0:T(8,128)}) %all-reduce.5.cloned.1.call-update) | async-done | bytes 262160 | tf_op jit(solution)/shard_map/psum | solution.py:9
  31.9 0.0 copy-done.4
  31.9 0.7 broadcast_select_fusion
  32.6 0.0 copy-start
  32.6 0.0 all-reduce.7.cloned.1.call-update
  32.6 0.0 all-reduce.9.cloned.1.call-start
  32.7 22.7 %all-reduce.7.cloned.1.call-done = f32[256,256]{1,0:T(8,128)} async-done(((f32[256,256]{1,0:T(8,128)}), f32[256,256]{1,0:T(8,128)}) %all-reduce.7.cloned.1.call-update) | async-done | bytes 262160 | tf_op jit(solution)/shard_map/psum | solution.py:9
  55.4 0.0 copy-done
  55.4 1.3 fusion.10
  56.7 0.0 copy-start.3
  56.7 0.0 all-reduce.9.cloned.1.call-update
  56.7 0.9 copy-done.3
  57.7 131.5 %all-reduce.9.cloned.1.call-done = f32[256,256]{0,1:T(8,128)} async-done(((f32[256,256]{0,1:T(8,128)}), f32[256,256]{0,1:T(8,128)}) %all-reduce.9.cloned.1.call-update) | async-done | bytes 262160 | tf_op jit(solution)/shard_map/psum | solution.py:36
  189.2 1.0 broadcast_multiply_fusion
  190.2 0.0 copy-start.2
  190.2 0.1 copy.7
  190.3 0.8 copy-done.2
  191.2 11.7 %cholesky.49 = f32[128,128]{1,0:T(8,128)S(1)} custom-call(f32[128,128]{1,0:T(8,128)S(1)} %cholesky.115), custom_call_target="Cholesky" | custom-call | tf_op jit(solution)/shard_map/jit(cholesky)/cholesky | solution.py:40
  203.0 9.8 %custom-call.15 = f32[1,128,128]{1,2,0:T(8,128)S(1)} custom-call(f32[1,128,128]{2,1,0:T(8,128)S(1)} %get-tuple-element.75), custom_call_target="InvertDiagBlocksLowerTriangular" | custom-call | tf_op jit(solution)/shard_map/jit(cholesky)/cholesky | solution.py:40
  212.8 0.2 constant_dynamic-update-slice_fusion.1
  213.0 0.3 convolution_subtract_fusion.3
  213.3 11.7 %cholesky.103 = f32[128,128]{1,0:T(8,128)S(1)} custom-call(f32[128,128]{1,0:T(8,128)S(1)} %convolution_subtract_fusion.3), custom_call_target="Cholesky" | custom-call | tf_op jit(solution)/shard_map/jit(cholesky)/cholesky | solution.py:40
  225.0 0.6 compare_reduce_fusion
  227.0 0.1 triangular_solve.57
  227.1 4.1 %while.1 = (s32[]{:T(128)}, f32[256,256]{1,0:T(8,128)S(1)}, s32[2,2]{1,0:T(2,128)S(1)}, f32[2,128,128]{2,1,0:T(8,128)S(1)}, s32[]{:T(128)}) while((s32[]{:T(128)}, f32[256,256]{1,0:T(8,128)S(1)}, s32[2,2]{1,0:T(2,128)S(1)}, f32[2,128,128]{2,1,0:T(8,128)S(1)}, s32[]{:T(128)}) %tuple.60), condition=%wide.while_cond, body=%wide.while_body.sunk | while | flops 2 | bytes 131189 | solution.py:41
  227.2 0.6 fusion.32
  227.8 1.4 bitcast_dynamic-update-slice_fusion.2
  229.2 0.6 fusion.32
  229.8 1.4 bitcast_dynamic-update-slice_fusion.2
  231.2 19.7 %custom-call.16 = f32[2,128,128]{1,2,0:T(8,128)S(1)} custom-call(f32[2,128,128]{2,1,0:T(8,128)S(1)} %get-tuple-element.57), custom_call_target="InvertDiagBlocksLowerTriangular" | custom-call | tf_op jit(solution)/shard_map/jit(_solve_triangular)/triangular_solve | solution.py:41
  250.9 0.3 fusion.7
  251.2 0.4 convolution_subtract_fusion.2
  251.6 0.3 fusion.12
  252.0 0.8 copy.8
  252.8 0.8 copy.9
  (16 shorter events, 0.3 us)
Async XLA Ops:
  7.2 1.0 copy-start.1
  7.2 24.7 %all-reduce.5.cloned.1.call-start = ((), (), s32[]{:S(2)}) async-start(), calls=%async_computation | async-start | bytes 524288 | tf_op jit(solution)/shard_map/psum | solution.py:9
  8.6 23.3 %copy-start.4 = (f32[1,1,2,256,256]{4,3,2,1,0:T(8,128)S(1)}, f32[1,1,2,256,256]{4,3,2,1,0:T(8,128)}, u32[]{:S(2)}) copy-start(f32[1,1,2,256,256]{4,3,2,1,0:T(8,128)} %param.14) | copy-start | bytes 1572868
  9.4 46.0 %all-reduce.7.cloned.1.call-start = ((), (), s32[]{:S(2)}) async-start(), calls=%async_computation.1 | async-start | bytes 524288 | tf_op jit(solution)/shard_map/psum | solution.py:9
  9.4 0.7 copy-start.5
  32.6 22.8 %copy-start = (f32[256,256]{1,0:T(8,128)S(1)}, f32[256,256]{1,0:T(8,128)}, u32[]{:S(2)}) copy-start(f32[256,256]{1,0:T(8,128)} %all-reduce.5.cloned.1.call-done) | copy-start | bytes 786436
  32.6 156.6 %all-reduce.9.cloned.1.call-start = ((), (), s32[]{:S(2)}) async-start(), calls=%async_computation.2 | async-start | bytes 524288 | tf_op jit(solution)/shard_map/psum | solution.py:36
  56.7 0.9 copy-start.3
  190.2 1.0 copy-start.2
Sparse Core Ops, SparseCore 0:
  10.9 20.9 all-reduce.4
  34.8 20.5 all-reduce.6
  61.5 127.7 all-reduce.8
where the time goes:
time: 261 us; the launch traced here: 260 us
  waiting for transfers between devices  174 us (67%)
  other arithmetic  56.2 us (22%)
  between operations  16.5 us (6%)
  local copies, waits for them, and re-layouts  9.83 us (4%)
  matrix products  3.18 us (1%)
    psum x1, waiting for transfers between devices, gram_sum(): return lax.psum(local, ('line', 'sec'))  132 us
    psum x2, waiting for transfers between devices, broadcast(): return lax.psum(jnp.where(mine, array, jnp.zeros_like(array)), axis)  42.6 us
    another operation x6, other arithmetic, upper_factor(): lower = jnp.linalg.cholesky(gram_sum(matrix) / total)  33.9 us
    another operation x2, other arithmetic, upper_factor(): normed = jax.scipy.linalg.solve_triangular(lower, matrix.T, lower=True).T  19.7 us
  transfers between devices with their start and end apart: 3, of which 3 were waited for; matrix products, arithmetic and copies ran while one was open for 0% of the time, Pallas kernels for 0%

commit v1 on v0

--- a/solution.py
+++ b/solution.py
@@ -4,9 +4,15 @@
 from jax.sharding import PartitionSpec as P
 
 
+def add_all(x, name):
+    parts = lax.all_gather(x, name, axis=0, tiled=False)
+    summed = parts.sum(axis=0)
+    return summed
+
+
 def broadcast(array, axis, root):
     mine = lax.axis_index(axis) == root
-    return lax.psum(jnp.where(mine, array, jnp.zeros_like(array)), axis)
+    return add_all(jnp.where(mine, array, jnp.zeros_like(array)), axis)
 
 
 def exact_dot(left, right):

time: 261 us -> 220 us (0.84)
  waiting for transfers between devices: 174 us -> 130 us
  blocking collectives: 0 us -> 5 us
    psum x2 -> x0, waiting for transfers between devices: 42.6 us -> none  [broadcast(): return lax.psum(jnp.where(mine, array, jnp.zeros_like(array)), axis)]
    all_gather x0 -> x2, blocking collectives: none -> 5 us  [add_all(): parts = lax.all_gather(x, name, axis=0, tiled=False)]
  transfers between devices with their start and end apart: 3 -> 1, of which waited for: 3 -> 1; matrix products, arithmetic and copies ran while one was open for 0% -> 0% of each run, Pallas kernels for 0% -> 0%
where the time goes in v1:
time: 220 us
  waiting for transfers between devices  130 us (59%)
  other arithmetic  54.8 us (25%)
  between operations  16.8 us (8%)
  local copies, waits for them, and re-layouts  9.97 us (5%)
  blocking collectives  5 us (2%)
  matrix products  3.17 us (1%)
    psum x1, waiting for transfers between devices, gram_sum(): return lax.psum(local, ('line', 'sec'))  130 us
    another operation x6, other arithmetic, upper_factor(): lower = jnp.linalg.cholesky(gram_sum(matrix) / total)  33.9 us
    another operation x2, other arithmetic, upper_factor(): normed = jax.scipy.linalg.solve_triangular(lower, matrix.T, lower=True).T  19.7 us
    unnamed x11, local copies, waits for them, and re-layouts  5.13 us
    all_gather x2, blocking collectives, add_all(): parts = lax.all_gather(x, name, axis=0, tiled=False)  5 us
  transfers between devices with their start and end apart: 1, of which 1 were waited for; matrix products, arithmetic and copies ran while one was open for 0% of the time, Pallas kernels for 0%

profile of v1, /device:TPU:0, one launch (start us, length us, event | category | flops | bytes accessed | tf_op | source)
XLA Modules:
  0.0 219.9 jit_solution(6540483129204124155)
XLA Ops:
  7.2 0.0 copy-start
  7.2 0.0 all-reduce.3.cloned.1.call-start
  7.2 1.0 copy.31
  8.2 0.0 copy-start.3
  8.2 0.7 copy-done.3
  8.9 0.6 fusion.18
  10.8 0.0 copy-done
  10.8 0.4 conditional.4
  10.8 0.4 fusion.19
  11.2 2.2 all-gather
  13.4 0.0 copy-start.2
  13.5 1.0 copy-done.2
  14.5 2.8 %all-gather.1 = f32[512,256]{1,0:T(8,128)S(1)} all-gather(f32[256,256]{1,0:T(8,128)S(1)} %broadcast_select_fusion), channel_id=3, replica_groups=mesh['line'=16,'sec'=2] {'sec'}, dimensions={0}, use_global_device_ids=true | all-gather | bytes 786432 | tf_op jit(solution)/shard_map/all_gather | solution.py:8
  17.4 1.3 fusion.10
  18.7 0.0 all-reduce.3.cloned.1.call-update
  18.8 129.8 %all-reduce.3.cloned.1.call-done = f32[256,256]{0,1:T(8,128)} async-done(((f32[256,256]{0,1:T(8,128)}), f32[256,256]{0,1:T(8,128)}) %all-reduce.3.cloned.1.call-update) | async-done | bytes 262160 | tf_op jit(solution)/shard_map/psum | solution.py:42
  148.6 1.0 broadcast_multiply_fusion
  149.6 0.0 copy-start.1
  149.6 0.1 copy.7
  149.7 0.8 copy-done.1
  150.6 11.7 %cholesky.49 = f32[128,128]{1,0:T(8,128)S(1)} custom-call(f32[128,128]{1,0:T(8,128)S(1)} %cholesky.115), custom_call_target="Cholesky" | custom-call | tf_op jit(solution)/shard_map/jit(cholesky)/cholesky | solution.py:46
  162.4 9.8 %custom-call.15 = f32[1,128,128]{1,2,0:T(8,128)S(1)} custom-call(f32[1,128,128]{2,1,0:T(8,128)S(1)} %get-tuple-element.75), custom_call_target="InvertDiagBlocksLowerTriangular" | custom-call | tf_op jit(solution)/shard_map/jit(cholesky)/cholesky | solution.py:46
  172.2 0.2 constant_dynamic-update-slice_fusion.1
  172.4 0.3 convolution_subtract_fusion.3
  172.7 11.7 %cholesky.103 = f32[128,128]{1,0:T(8,128)S(1)} custom-call(f32[128,128]{1,0:T(8,128)S(1)} %convolution_subtract_fusion.3), custom_call_target="Cholesky" | custom-call | tf_op jit(solution)/shard_map/jit(cholesky)/cholesky | solution.py:46
  184.4 0.6 compare_reduce_fusion
  186.4 0.1 triangular_solve.57
  186.5 4.1 %while.1 = (s32[]{:T(128)}, f32[256,256]{1,0:T(8,128)S(1)}, s32[2,2]{1,0:T(2,128)S(1)}, f32[2,128,128]{2,1,0:T(8,128)S(1)}, s32[]{:T(128)}) while((s32[]{:T(128)}, f32[256,256]{1,0:T(8,128)S(1)}, s32[2,2]{1,0:T(2,128)S(1)}, f32[2,128,128]{2,1,0:T(8,128)S(1)}, s32[]{:T(128)}) %tuple.60), condition=%wide.while_cond, body=%wide.while_body.sunk | while | flops 2 | bytes 131189 | solution.py:47
  186.6 0.6 fusion.32
  187.2 1.4 bitcast_dynamic-update-slice_fusion.2
  188.6 0.6 fusion.32
  189.2 1.4 bitcast_dynamic-update-slice_fusion.2
  190.6 19.7 %custom-call.16 = f32[2,128,128]{1,2,0:T(8,128)S(1)} custom-call(f32[2,128,128]{2,1,0:T(8,128)S(1)} %get-tuple-element.57), custom_call_target="InvertDiagBlocksLowerTriangular" | custom-call | tf_op jit(solution)/shard_map/jit(_solve_triangular)/triangular_solve | solution.py:47
  210.3 0.3 fusion.7
  210.6 0.4 convolution_subtract_fusion.2
  211.0 0.3 fusion.12
  211.4 0.8 copy.8
  212.2 0.8 copy.9
  (20 shorter events, 0.4 us)
Async XLA Ops:
  7.2 3.6 %copy-start = (f32[1,1,256,256]{3,2,1,0:T(8,128)S(1)}, f32[1,1,256,256]{3,2,1,0:T(8,128)}, u32[]{:S(2)}) copy-start(f32[1,1,256,256]{3,2,1,0:T(8,128)} %param.13) | copy-start | bytes 786436
  7.2 141.5 %all-reduce.3.cloned.1.call-start = ((), (), s32[]{:S(2)}) async-start(), calls=%async_computation | async-start | bytes 524288 | tf_op jit(solution)/shard_map/psum | solution.py:42
  8.2 0.7 copy-start.3
  13.4 1.0 copy-start.2
  149.6 1.0 copy-start.1
Sparse Core Ops, SparseCore 0:
  18.8 129.7 all-reduce.2
